TPU v7x, 32 devices: a whole 2x2x4 slice. The times are simulated.
32 devices in a mesh: req: 2 (over y), ctx: 16 (over z, x, core).
Axes of the slice: x: 2, y: 2, z: 4, core: 2. Of those that a mesh axis runs over, the one named last changes fastest.
Arguments:
- query_source: bfloat16 [2304, 256], P(('req', 'ctx')), parts along dimension 0, may hold values from -32 to 32
- key_source: bfloat16 [2304, 256], P(('req', 'ctx')), parts along dimension 0, may hold values from -4 to 4
- query_edit: bfloat16 [2304, 256], P(('req', 'ctx')), parts along dimension 0, may hold values from -32 to 32
- key_edit: bfloat16 [2304, 256], P(('req', 'ctx')), parts along dimension 0, may hold values from -4 to 4
- text_count: int32 [2], P('req'), parts along dimension 0, may hold values from 72 to 288, as said below
Outputs:
- query_grad: float32 [2304, 256], P(('req', 'ctx')), parts along dimension 0
- key_grad: float32 [2304, 256], P(('req', 'ctx')), parts along dimension 0
There are 2 independent parts, one for each index of `req`. A program takes and returns all parts, laid end to end along the dimension named above; each array names one. Nothing has to cross between parts.
Inputs may be any that keep to these rules, and one draw needn't show every extreme that they name: The first 288 positions are text slots; those at or past text_count are padding.
All inputs are finite; a program needn't handle non-finite values.
Results may differ from a plain program's by a relative error of at most 0.0095.
Values may be sent and summed in bfloat16 or wider, within the bound.
A program may use at most 64 MiB of HBM per device.

v0:
```python
import math

import jax
import jax.numpy as jnp
from jax import lax
from jax.sharding import PartitionSpec as P

HEAD_DIM = 128


def masked_softmax(scores, key_valid):
    masked = jnp.where(key_valid, scores, -jnp.inf)
    highest = jnp.max(masked, axis=-1, keepdims=True)
    powers = jnp.where(key_valid, jnp.exp(scores - highest), 0.0)
    totals = jnp.sum(powers, axis=-1, keepdims=True)
    return (powers / totals, highest + jnp.log(totals))


def local(query_source, key_source, query_edit, key_edit, text_count):
    local_rows, full_width = query_source.shape
    head_count = full_width // HEAD_DIM
    all_rows = local_rows * lax.axis_size("ctx")
    text_slots = min(512, all_rows // 4)
    score_scale = 1.0 / math.sqrt(HEAD_DIM)
    weight = 4.0 * all_rows * math.sqrt(all_rows)
    places = jnp.arange(all_rows)
    token_valid = (places >= text_slots) | (places < text_count[0])
    own_places = lax.axis_index("ctx") * local_rows + jnp.arange(local_rows)
    own_valid = (own_places >= text_slots) | (own_places < text_count[0])
    own_weight = own_valid.astype(jnp.float32)

    def heads_view(matrix):
        return matrix.reshape(matrix.shape[0], head_count, HEAD_DIM)

    every_ks, every_ke = (
        lax.all_gather(key_source, "ctx", axis=0, tiled=True),
        lax.all_gather(key_edit, "ctx", axis=0, tiled=True),
    )
    own_qs = heads_view(query_source)
    own_qe = heads_view(query_edit)
    scores_source = (
        jnp.einsum("rhd,lhd->hrl", own_qs, heads_view(every_ks), preferred_element_type=jnp.float32)
        * score_scale
    )
    scores_edit = (
        jnp.einsum("rhd,lhd->hrl", own_qe, heads_view(every_ke), preferred_element_type=jnp.float32)
        * score_scale
    )
    probs_source, logsum_source = masked_softmax(scores_source, token_valid[None, None, :])
    probs_edit, logsum_edit = masked_softmax(scores_edit, token_valid[None, None, :])
    map_grad = 2.0 * weight * (probs_edit - probs_source) * own_weight[None, :, None]
    row_delta = jnp.sum(map_grad * probs_edit, axis=-1, keepdims=True)
    score_grad = (probs_edit * (map_grad - row_delta)).astype(jnp.bfloat16)
    query_grad = (
        jnp.einsum(
            "hrl,lhd->rhd", score_grad, heads_view(every_ke), preferred_element_type=jnp.float32
        )
        * score_scale
    )
    term_block = (
        jnp.einsum("hrl,rhd->lhd", score_grad, own_qe, preferred_element_type=jnp.float32)
        * score_scale
    )
    key_grad = lax.psum_scatter(
        term_block.reshape(local_rows * lax.axis_size("ctx"), full_width),
        "ctx",
        scatter_dimension=0,
        tiled=True,
    )
    return (query_grad.reshape(local_rows, full_width), key_grad)


def solution(mesh):
    in_specs = (
        P(("req", "ctx"), None),
        P(("req", "ctx"), None),
        P(("req", "ctx"), None),
        P(("req", "ctx"), None),
        P("req"),
    )
    out_specs = (P(("req", "ctx"), None), P(("req", "ctx"), None))
    return jax.shard_map(local, mesh=mesh, in_specs=in_specs, out_specs=out_specs, check_vma=False)
```

profile of v0, /device:TPU:0, one launch (start us, length us, event | category | flops | bytes accessed | tf_op | source)
XLA Modules:
  0.0 119.5 jit_solution(7638093069102241119)
XLA Ops:
  7.2 0.0 copy-start
  7.2 0.0 copy-start.1
  7.2 0.0 reduce-scatter.2.cloned.1.call-start
  7.9 25.1 %all_gather.7 = bf16[1152,256]{1,0:T(8,128)(2,1)S(1)} all-gather(bf16[72,256]{1,0:T(8,128)(2,1)} %param.6), channel_id=1, replica_groups=mesh['req'=2,'ctx'=16] {'ctx'}, dimensions={0}, use_global_device_ids=true | all-gather | bytes 626688 | tf_op jit(solution)/shard_map/all_gather | solution.py:36
  33.0 0.3 copy.24
  33.3 0.0 copy-done.1
  33.3 0.0 copy-start.2
  33.3 19.1 %all_gather.6 = bf16[1152,256]{1,0:T(8,128)(2,1)S(1)} all-gather(bf16[72,256]{1,0:T(8,128)(2,1)S(1)} %copy-done.1), channel_id=1, replica_groups=mesh['req'=2,'ctx'=16] {'ctx'}, dimensions={0}, use_global_device_ids=true | all-gather | bytes 626688 | tf_op jit(solution)/shard_map/all_gather | solution.py:37
  52.4 0.3 copy.21
  52.7 0.0 copy-done.2
  52.7 0.2 convolution_multiply_fusion.1
  52.9 0.0 copy-done
  53.0 0.2 convolution_multiply_fusion.2
  53.2 0.3 fusion.33
  53.5 0.5 multiply_reduce_fusion
  54.0 0.2 multiply_convert_fusion
  54.2 0.4 convolution_multiply_fusion
  54.5 1.4 %copy.30 = f32[1152,256]{1,0:T(8,128)} copy(f32[1152,256]{0,1:T(8,128)S(1)} %bitcast.40) | data formatting | bytes 2359296 | tf_op jit(solution)/shard_map/reshape | solution.py:65
  55.9 0.0 reduce-scatter.2.cloned.1.call-update
  55.9 0.4 fusion.12
  56.3 0.6 copy.50
  56.9 55.7 %reduce-scatter.2.cloned.1.call-done = f32[72,256]{1,0:T(8,128)} async-done(((f32[1152,256]{1,0:T(8,128)}), f32[72,256]{1,0:T(8,128)}) %reduce-scatter.2.cloned.1.call-update) | async-done | bytes 73744 | tf_op jit(solution)/shard_map/reduce_scatter | solution.py:64
  (2 shorter events, 0.0 us)
Async XLA Ops:
  7.2 45.8 %copy-start = (bf16[72,256]{1,0:T(8,128)(2,1)S(1)}, bf16[72,256]{1,0:T(8,128)(2,1)}, u32[]{:S(2)}) copy-start(bf16[72,256]{1,0:T(8,128)(2,1)} %param.7) | copy-start | bytes 110596
  7.2 26.1 %copy-start.1 = (bf16[72,256]{1,0:T(8,128)(2,1)S(1)}, bf16[72,256]{1,0:T(8,128)(2,1)}, u32[]{:S(2)}) copy-start(bf16[72,256]{1,0:T(8,128)(2,1)} %param.8) | copy-start | bytes 110596
  7.2 105.5 %reduce-scatter.2.cloned.1.call-start = ((), (), s32[]{:S(2)}) async-start(), calls=%async_computation.1 | async-start | bytes 1253376 | tf_op jit(solution)/shard_map/reduce_scatter | solution.py:64
  33.3 19.4 %copy-start.2 = (bf16[72,256]{1,0:T(8,128)(2,1)S(1)}, bf16[72,256]{1,0:T(8,128)(2,1)}, u32[]{:S(2)}) copy-start(bf16[72,256]{1,0:T(8,128)(2,1)} %param.5) | copy-start | bytes 110596
Sparse Core Ops, SparseCore 0:
  56.1 56.5 reduce-scatter.1
where the time goes:
time: 120 us
  waiting for transfers between devices  55.7 us (46%)
  blocking collectives  44.1 us (37%)
  between operations  14.8 us (12%)
  local copies, waits for them, and re-layouts  2.63 us (2%)
  matrix products  1.21 us (1%)
    reduce_scatter x1, waiting for transfers between devices, local(): lax.psum_scatter(term_block.reshape(local_rows * lax.axis_size('ctx'), fu...  55.7 us
    all_gather x1, blocking collectives, local(): lax.all_gather(key_source, 'ctx', axis=0, tiled=True)  25.1 us
    all_gather x1, blocking collectives, local(): lax.all_gather(key_edit, 'ctx', axis=0, tiled=True)  19.1 us
  transfers between devices with their start and end apart: 1, of which 1 were waited for; matrix products, arithmetic and copies ran while one was open for 1% of the time, Pallas kernels for 0%

commit v1 on v0

v1 whole, which is shorter than its diff:
```python
import functools
import math

import jax
import jax.numpy as jnp
from jax import lax
from jax.experimental import pallas as pl
from jax.experimental.pallas import tpu as pltpu
from jax.sharding import PartitionSpec as P

HEAD_DIM = 128
MASKED = -1e30
SQUARE = False
F32 = jnp.float32
BF16 = jnp.bfloat16


def kernel(
    chips,
    count_ref, qs_hbm, ks_hbm, qe_hbm, ke_hbm,
    qg_ref, kg_ref,
    krecv, kother, qrecv, qother, e_buf, s_buf, m_buf, st_send, st_recv,
    kg_send, kg_recv, qg_send, qg_recv, kg_own, qg_own,
    load_sem, ksend_sem, krecv_sem, qsend_sem, qrecv_sem, st_sems,
    kgsend_sem, kgrecv_sem, qgsend_sem, qgrecv_sem,
):
    members = chips // 2
    rows = krecv.shape[3]
    all_rows = rows * chips * 2
    text_slots = min(512, all_rows // 4)
    scale = 1.0 / math.sqrt(HEAD_DIM)
    weight = 4.0 * all_rows * math.sqrt(all_rows)
    me = lax.axis_index("ctx")
    chip, core = me // 2, me % 2
    other = 1 - core

    if SQUARE:
        group, member = chip // members, chip % members
        chip_of = lambda g, m: g * members + m
    else:
        group, member = chip % 2, chip // 2
        chip_of = lambda g, m: m * 2 + g

    def dev(g, m, c):
        return {"ctx": chip_of(g, m) * 2 + c}

    def shifted(d):
        return (member + d) % members

    def each(n, body, init):
        if n <= 8:
            for i in range(n):
                init = body(i, init)
            return init
        return lax.fori_loop(0, n, body, init)

    own_cols = pl.ds(pl.multiple_of(core * HEAD_DIM, HEAD_DIM), HEAD_DIM)
    other_cols = pl.ds(pl.multiple_of(other * HEAD_DIM, HEAD_DIM), HEAD_DIM)
    loads = []
    for i, (src, dst_own, dst_other) in enumerate((
        (ks_hbm, krecv.at[member, core, 0], kother.at[0]),
        (ke_hbm, krecv.at[member, core, 1], kother.at[1]),
        (qs_hbm, qrecv.at[group, core, 0], qother.at[0]),
        (qe_hbm, qrecv.at[group, core, 1], qother.at[1]),
    )):
        loads.append(pltpu.make_async_copy(src.at[:, own_cols], dst_own, load_sem.at[2 * i]))
        loads.append(pltpu.make_async_copy(src.at[:, other_cols], dst_other, load_sem.at[2 * i + 1]))
    for load in loads:
        load.start()

    barrier = pltpu.get_barrier_semaphore()

    def greet(d, carry):
        for c in (0, 1):
            pl.semaphore_signal(barrier, inc=1, device_id=dev(group, shifted(d + 1), c))
        return carry

    for c in (0, 1):
        pl.semaphore_signal(barrier, inc=1, device_id=dev(1 - group, member, c))
    pl.semaphore_signal(barrier, inc=1, device_id=dev(group, member, other))
    each(members - 1, greet, 0)
    pl.semaphore_wait(barrier, 2 * members + 1)
    for load in loads:
        load.wait()

    def key_copy(m, c, same):
        return pltpu.make_async_remote_copy(
            src_ref=krecv.at[member, core] if same else kother,
            dst_ref=krecv.at[member, core],
            send_sem=ksend_sem.at[m, c],
            recv_sem=krecv_sem.at[member, core],
            device_id=dev(group, m, c),
        )

    def key_arrival(m, c):
        return pltpu.make_async_remote_copy(
            src_ref=kother,
            dst_ref=krecv.at[m, c],
            send_sem=ksend_sem.at[m, c],
            recv_sem=krecv_sem.at[m, c],
            device_id=dev(group, m, c),
        )

    def query_copy(g, c, same):
        return pltpu.make_async_remote_copy(
            src_ref=qrecv.at[group, core] if same else qother,
            dst_ref=qrecv.at[group, core],
            send_sem=qsend_sem.at[g, c],
            recv_sem=qrecv_sem.at[group, core],
            device_id=dev(g, member, c),
        )

    def query_arrival(g, c):
        return pltpu.make_async_remote_copy(
            src_ref=qother,
            dst_ref=qrecv.at[g, c],
            send_sem=qsend_sem.at[g, c],
            recv_sem=qrecv_sem.at[g, c],
            device_id=dev(g, member, c),
        )

    query_copy(1 - group, core, True).start()
    query_copy(1 - group, other, False).start()
    query_copy(group, other, False).start()
    key_copy(member, other, False).start()

    def send_keys(d, carry):
        m = shifted(d + 1)
        key_copy(m, core, True).start()
        key_copy(m, other, False).start()
        return carry

    each(members - 1, send_keys, 0)

    count = count_ref[0]

    def valid(positions):
        return (positions >= text_slots) | (positions < count)

    query_arrival(group, other).wait_recv()
    query_arrival(1 - group, core).wait_recv()
    query_arrival(1 - group, other).wait_recv()

    def queries(which):
        pieces = [qrecv[g, c, which].astype(F32) for g in (0, 1) for c in (0, 1)]
        return jnp.concatenate(pieces, axis=0).astype(BF16)

    q_source, q_edit = queries(0), queries(1)
    width = 4 * rows
    lane = lax.broadcasted_iota(jnp.int32, (1, width), 1)
    piece = lane // rows
    lane_chip = jnp.where(piece < 2, chip_of(0, member), chip_of(1, member))
    row_place = (lane_chip * 2 + piece % 2) * rows + lane % rows
    row_weight = jnp.where(valid(row_place), 2.0 * weight, 0.0)

    def keys(m, which):
        pieces = [krecv[m, c, which].astype(F32) for c in (0, 1)]
        return jnp.concatenate(pieces, axis=0).astype(BF16)

    def merge(a, b):
        me1, le1, ms1, ls1, sq1, cr1 = a
        me2, le2, ms2, ls2, sq2, cr2 = b
        m_e, m_s = jnp.maximum(me1, me2), jnp.maximum(ms1, ms2)
        fe1, fe2 = jnp.exp(me1 - m_e), jnp.exp(me2 - m_e)
        fs1, fs2 = jnp.exp(ms1 - m_s), jnp.exp(ms2 - m_s)
        return (
            m_e, le1 * fe1 + le2 * fe2,
            m_s, ls1 * fs1 + ls2 * fs2,
            sq1 * fe1 * fe1 + sq2 * fe2 * fe2,
            cr1 * fe1 * fs1 + cr2 * fe2 * fs2,
        )

    def powers(m, which, q, key_valid, buf):
        scores = lax.dot_general(
            keys(m, which), q, (((1,), (1,)), ((), ())), preferred_element_type=F32
        ) * scale
        scores = jnp.where(key_valid, scores, MASKED)
        top = jnp.max(scores, axis=0, keepdims=True)
        power = jnp.where(key_valid, jnp.exp(scores - top), 0.0)
        buf[m] = power
        m_buf[m, which:which + 1] = top
        return top, power, jnp.sum(power, axis=0, keepdims=True)

    def score_chunk(m, stats):
        place = chip_of(group, m) * (2 * rows) + lax.broadcasted_iota(jnp.int32, (2 * rows, 1), 0)
        key_valid = valid(place)
        m_s, s_pow, l_s = powers(m, 0, q_source, key_valid, s_buf)
        m_e, e_pow, l_e = powers(m, 1, q_edit, key_valid, e_buf)
        sq = jnp.sum(e_pow * e_pow, axis=0, keepdims=True)
        cr = jnp.sum(e_pow * s_pow, axis=0, keepdims=True)
        new = (m_e, l_e, m_s, l_s, sq, cr)
        return new if stats is None else merge(stats, new)

    key_arrival(member, other).wait_recv()
    stats = score_chunk(member, None)

    def far_chunk(d, stats):
        m = shifted(members - 1 - d)
        key_arrival(m, core).wait_recv()
        key_arrival(m, other).wait_recv()
        return score_chunk(m, stats)

    stats = each(members - 1, far_chunk, stats)

    for i, value in enumerate(stats):
        st_send[i:i + 1] = value
    for i in (6, 7):
        st_send[i:i + 1] = jnp.zeros((1, width), F32)
    stat_copy = pltpu.make_async_remote_copy(
        src_ref=st_send, dst_ref=st_recv, send_sem=st_sems.at[0], recv_sem=st_sems.at[1],
        device_id=dev(1 - group, member, core),
    )
    stat_copy.start()
    stat_copy.wait_recv()
    m_e, l_e, m_s, l_s, sq, cr = merge(stats, tuple(st_recv[i:i + 1] for i in range(6)))
    inv_e, inv_s = 1.0 / l_e, 1.0 / l_s
    delta = row_weight * (sq * inv_e * inv_e - cr * inv_e * inv_s)

    def kg_copy(m, c):
        return pltpu.make_async_remote_copy(
            src_ref=kg_send.at[m, c], dst_ref=kg_recv.at[member, core],
            send_sem=kgsend_sem.at[m, c], recv_sem=kgrecv_sem.at[member, core],
            device_id=dev(group, m, c),
        )

    def kg_arrival(m, c):
        return pltpu.make_async_remote_copy(
            src_ref=kg_send.at[m, c], dst_ref=kg_recv.at[m, c],
            send_sem=kgsend_sem.at[m, c], recv_sem=kgrecv_sem.at[m, c],
            device_id=dev(group, m, c),
        )

    def qg_copy(g, c):
        return pltpu.make_async_remote_copy(
            src_ref=qg_send.at[g, c], dst_ref=qg_recv.at[group, core],
            send_sem=qgsend_sem.at[g, c], recv_sem=qgrecv_sem.at[group, core],
            device_id=dev(g, member, c),
        )

    def qg_arrival(g, c):
        return pltpu.make_async_remote_copy(
            src_ref=qg_send.at[g, c], dst_ref=qg_recv.at[g, c],
            send_sem=qgsend_sem.at[g, c], recv_sem=qgrecv_sem.at[g, c],
            device_id=dev(g, member, c),
        )

    def grad_chunk(m, q_total):
        prob_e = e_buf[m] * (jnp.exp(m_buf[m, 1:2] - m_e) * inv_e)
        prob_s = s_buf[m] * (jnp.exp(m_buf[m, 0:1] - m_s) * inv_s)
        grad = (prob_e * (row_weight * (prob_e - prob_s) - delta)).astype(BF16)
        k_part = jnp.dot(grad, q_edit, preferred_element_type=F32) * scale
        q_part = lax.dot_general(
            keys(m, 1), grad, (((0,), (0,)), ((), ())), preferred_element_type=F32
        )
        return k_part, q_part if q_total is None else q_total + q_part

    def far_grad(d, q_total):
        m = shifted(members - 1 - d)
        k_part, q_total = grad_chunk(m, q_total)
        for c in (0, 1):
            kg_send[m, c] = k_part[c * rows:(c + 1) * rows].astype(BF16)
            kg_copy(m, c).start()
        return q_total

    q_total = each(members - 1, far_grad, jnp.zeros((HEAD_DIM, width), F32))
    k_part, q_total = grad_chunk(member, q_total)
    for c in (0, 1):
        kg_own[c] = k_part[c * rows:(c + 1) * rows]
    kg_send[member, other] = kg_own[other].astype(BF16)
    kg_copy(member, other).start()

    q_rows = q_total.T * scale
    for g in (0, 1):
        for c in (0, 1):
            part = q_rows[(2 * g + c) * rows:(2 * g + c + 1) * rows]
            qg_own[g, c] = part
            qg_send[g, c] = part.astype(BF16)
    qg_copy(1 - group, core).start()
    qg_copy(1 - group, other).start()
    qg_copy(group, other).start()

    def put(ref, mine, theirs):
        ref[:, :HEAD_DIM] = jnp.where(core == 0, mine, theirs)
        ref[:, HEAD_DIM:] = jnp.where(core == 0, theirs, mine)

    kg_arrival(member, other).wait_recv()

    def add_far(d, sums):
        mine, theirs = sums
        m = shifted(d + 1)
        kg_arrival(m, core).wait_recv()
        kg_arrival(m, other).wait_recv()
        return mine + kg_recv[m, core].astype(F32), theirs + kg_recv[m, other].astype(F32)

    sums = each(members - 1, add_far, (kg_own[core], kg_recv[member, other].astype(F32)))
    put(kg_ref, *sums)

    qg_arrival(group, other).wait_recv()
    qg_arrival(1 - group, core).wait_recv()
    qg_arrival(1 - group, other).wait_recv()
    put(
        qg_ref,
        qg_own[group, core] + qg_recv[1 - group, core].astype(F32),
        qg_recv[group, other].astype(F32) + qg_recv[1 - group, other].astype(F32),
    )

    def drain(d, carry):
        m = shifted(d + 1)
        for c in (0, 1):
            key_copy(m, c, False).wait_send()
            kg_copy(m, c).wait_send()
        return carry

    each(members - 1, drain, 0)
    key_copy(member, other, False).wait_send()
    kg_copy(member, other).wait_send()
    for copy in (query_copy(1 - group, core, True), query_copy(1 - group, other, False),
                 query_copy(group, other, False), qg_copy(1 - group, core),
                 qg_copy(1 - group, other), qg_copy(group, other), stat_copy):
        copy.wait_send()


def solution(mesh):
    chips = mesh.shape["ctx"] // 2
    members = chips // 2

    def local(query_source, key_source, query_edit, key_edit, text_count):
        rows, full = query_source.shape
        width = 4 * rows
        dma = pltpu.SemaphoreType.DMA
        vmem = pltpu.VMEM
        any_spec = pl.BlockSpec(memory_space=pl.ANY)
        return pl.pallas_call(
            functools.partial(kernel, chips),
            out_shape=(
                jax.ShapeDtypeStruct((rows, full), F32),
                jax.ShapeDtypeStruct((rows, full), F32),
            ),
            in_specs=[pl.BlockSpec(memory_space=pltpu.SMEM)] + [any_spec] * 4,
            out_specs=(pl.BlockSpec(memory_space=pltpu.VMEM),) * 2,
            scratch_shapes=[
                vmem((members, 2, 2, rows, HEAD_DIM), BF16),
                vmem((2, rows, HEAD_DIM), BF16),
                vmem((2, 2, 2, rows, HEAD_DIM), BF16),
                vmem((2, rows, HEAD_DIM), BF16),
                vmem((members, 2 * rows, width), F32),
                vmem((members, 2 * rows, width), F32),
                vmem((members, 8, width), F32),
                vmem((8, width), F32),
                vmem((8, width), F32),
                vmem((members, 2, rows, HEAD_DIM), BF16),
                vmem((members, 2, rows, HEAD_DIM), BF16),
                vmem((2, 2, rows, HEAD_DIM), BF16),
                vmem((2, 2, rows, HEAD_DIM), BF16),
                vmem((2, rows, HEAD_DIM), F32),
                vmem((2, 2, rows, HEAD_DIM), F32),
                dma((8,)),
                dma((members, 2)),
                dma((members, 2)),
                dma((2, 2)),
                dma((2, 2)),
                dma((2,)),
                dma((members, 2)),
                dma((members, 2)),
                dma((2, 2)),
                dma((2, 2)),
            ],
            compiler_params=pltpu.CompilerParams(collective_id=0, has_side_effects=True),
        )(text_count, query_source, key_source, query_edit, key_edit)

    spec = P(("req", "ctx"), None)
    return jax.shard_map(
        local, mesh=mesh, in_specs=(spec,) * 4 + (P("req"),), out_specs=(spec, spec), check_vma=False
    )
```

time: 120 us -> 26.6 us (0.22)
  waiting for transfers between devices: 55.7 us -> 0 us
  blocking collectives: 44.1 us -> 0 us
  Pallas kernels: 0 us -> 22.9 us
  between operations: 14.8 us -> 1.29 us
  matrix products: 1.21 us -> 0 us
    reduce_scatter x1 -> x0, waiting for transfers between devices: 55.7 us -> none  [local(): lax.psum_scatter(term_block.reshape(local_rows * lax.axis_size('ctx'), fu...]
    all_gather x2 -> x0, blocking collectives: 44.1 us -> none  [the longest x1 25.1 us: local(): lax.all_gather(key_source, 'ctx', axis=0, tiled=True)]
    pallas_call x0 -> x1, Pallas kernels: none -> 22.9 us  [local(): pl.pallas_call(functools.partial(kernel, chips), out_shape=(jax.ShapeDtyp...]
    unnamed x6 -> x4, local copies, waits for them, and re-layouts: 0.02 us -> 2.19 us
    reshape x2 -> x0, local copies, waits for them, and re-layouts: 2.02 us -> none  [the longest x1 1.38 us: local(): term_block.reshape(local_rows * lax.axis_size('ctx'), full_width)]
    dot_general x4 -> x0, matrix products: 1.21 us -> none  [the longest x1 0.36 us: local(): jnp.einsum('hrl,rhd->lhd', score_grad, own_qe, preferred_element_type=jnp...]
  transfers between devices with their start and end apart: 1 -> 0, of which waited for: 1 -> 0; matrix products, arithmetic and copies ran while one was open for 1% -> 0% of each run, Pallas kernels for 0% -> 0%
where the time goes in v1:
time: 26.6 us; the launch traced here: 26.4 us
  Pallas kernels  22.9 us (86%)
  local copies, waits for them, and re-layouts  2.19 us (8%)
  between operations  1.29 us (5%)
    pallas_call x1, Pallas kernels, local(): pl.pallas_call(functools.partial(kernel, chips), out_shape=(jax.ShapeDtyp...  22.9 us
    unnamed x4, local copies, waits for them, and re-layouts  2.19 us

profile of v1, /device:TPU:0, one launch (start us, length us, event | category | flops | bytes accessed | tf_op | source)
XLA Modules:
  0.0 26.4 jit_solution(13413501415267550455)
XLA Ops:
  1.3 22.9 %shard_map.68 = (f32[72,256]{1,0:T(8,128)}, f32[72,256]{1,0:T(8,128)}) custom-call(s32[1]{0:T(128)S(6)} %copy.9.count_ref, bf16[72,256]{1,0:T(8,128)(2,1)} %qs_hbm.1, bf16[72,256]{1,0:T(8,128)(2,1)} %ks_hbm.1, bf16[72,256]{1,0:T(8,128)(2,1)} %qe_hbm.1, bf16[72,256]{1,0:T(8,128)(2,1)} %ke_hbm.1), custom_call_target="tpu_custom_call" | custom-call | tf_op jit(solution)/shard_map/pallas_call | solution.py:333
  24.2 0.0 copy-start
  24.2 1.6 %copy.10 = f32[72,256]{1,0:T(8,128)} copy(f32[72,256]{1,0:T(8,128)} %get-tuple-element.4) | data formatting | bytes 147456
  25.8 0.0 copy-done
  25.8 0.6 %copy.11 = f32[72,256]{1,0:T(8,128)} copy(f32[72,256]{1,0:T(8,128)S(1)} %copy-done) | data formatting | bytes 147456
Async XLA Ops:
  24.2 1.6 %copy-start = (f32[72,256]{1,0:T(8,128)S(1)}, f32[72,256]{1,0:T(8,128)}, u32[]{:S(2)}) copy-start(f32[72,256]{1,0:T(8,128)} %get-tuple-element.5) | copy-start | bytes 221188

commit v2 on v1

--- a/solution.py
+++ b/solution.py
@@ -10,7 +10,7 @@
 
 HEAD_DIM = 128
 MASKED = -1e30
-SQUARE = False
+SQUARE = True
 F32 = jnp.float32
 BF16 = jnp.bfloat16
 

time: 26.6 us -> 24.8 us (0.932)
  Pallas kernels: 22.9 us -> 21.1 us
    pallas_call x1, Pallas kernels: 22.9 us -> 21.1 us  [local(): pl.pallas_call(functools.partial(kernel, chips), out_shape=(jax.ShapeDtyp...]
where the time goes in v2:
time: 24.8 us; the launch traced here: 24.6 us
  Pallas kernels  21.1 us (85%)
  local copies, waits for them, and re-layouts  2.19 us (9%)
  between operations  1.29 us (5%)
    pallas_call x1, Pallas kernels, local(): pl.pallas_call(functools.partial(kernel, chips), out_shape=(jax.ShapeDtyp...  21.1 us
    unnamed x4, local copies, waits for them, and re-layouts  2.19 us

profile of v2, /device:TPU:0, one launch (start us, length us, event | category | flops | bytes accessed | tf_op | source)
XLA Modules:
  0.0 24.6 jit_solution(15312662116981504783)
XLA Ops:
  1.3 21.1 %shard_map.68 = (f32[72,256]{1,0:T(8,128)}, f32[72,256]{1,0:T(8,128)}) custom-call(s32[1]{0:T(128)S(6)} %copy.9.count_ref, bf16[72,256]{1,0:T(8,128)(2,1)} %qs_hbm.1, bf16[72,256]{1,0:T(8,128)(2,1)} %ks_hbm.1, bf16[72,256]{1,0:T(8,128)(2,1)} %qe_hbm.1, bf16[72,256]{1,0:T(8,128)(2,1)} %ke_hbm.1), custom_call_target="tpu_custom_call" | custom-call | tf_op jit(solution)/shard_map/pallas_call | solution.py:333
  22.4 0.0 copy-start
  22.4 1.6 %copy.10 = f32[72,256]{1,0:T(8,128)} copy(f32[72,256]{1,0:T(8,128)} %get-tuple-element.4) | data formatting | bytes 147456
  23.9 0.0 copy-done
  24.0 0.6 %copy.11 = f32[72,256]{1,0:T(8,128)} copy(f32[72,256]{1,0:T(8,128)S(1)} %copy-done) | data formatting | bytes 147456
Async XLA Ops:
  22.4 1.6 %copy-start = (f32[72,256]{1,0:T(8,128)S(1)}, f32[72,256]{1,0:T(8,128)}, u32[]{:S(2)}) copy-start(f32[72,256]{1,0:T(8,128)} %get-tuple-element.5) | copy-start | bytes 221188

commit v3 on v2

--- a/solution.py
+++ b/solution.py
@@ -17,9 +17,9 @@
 
 def kernel(
     chips,
-    count_ref, qs_hbm, ks_hbm, qe_hbm, ke_hbm,
+    count_hbm, qs_hbm, ks_hbm, qe_hbm, ke_hbm,
     qg_ref, kg_ref,
-    krecv, kother, qrecv, qother, e_buf, s_buf, m_buf, st_send, st_recv,
+    count_ref, krecv, kother, qrecv, qother, e_buf, s_buf, m_buf, st_send, st_recv,
     kg_send, kg_recv, qg_send, qg_recv, kg_own, qg_own,
     load_sem, ksend_sem, krecv_sem, qsend_sem, qrecv_sem, st_sems,
     kgsend_sem, kgrecv_sem, qgsend_sem, qgrecv_sem,
@@ -65,6 +65,7 @@
     )):
         loads.append(pltpu.make_async_copy(src.at[:, own_cols], dst_own, load_sem.at[2 * i]))
         loads.append(pltpu.make_async_copy(src.at[:, other_cols], dst_other, load_sem.at[2 * i + 1]))
+    loads.append(pltpu.make_async_copy(count_hbm, count_ref, load_sem.at[8]))
     for load in loads:
         load.start()
 
@@ -333,12 +334,13 @@
         return pl.pallas_call(
             functools.partial(kernel, chips),
             out_shape=(
-                jax.ShapeDtypeStruct((rows, full), F32),
-                jax.ShapeDtypeStruct((rows, full), F32),
+                pltpu.VMEM((rows, full), F32),
+                pltpu.VMEM((rows, full), F32),
             ),
-            in_specs=[pl.BlockSpec(memory_space=pltpu.SMEM)] + [any_spec] * 4,
+            in_specs=[any_spec] * 5,
             out_specs=(pl.BlockSpec(memory_space=pltpu.VMEM),) * 2,
             scratch_shapes=[
+                pltpu.SMEM((1,), jnp.int32),
                 vmem((members, 2, 2, rows, HEAD_DIM), BF16),
                 vmem((2, rows, HEAD_DIM), BF16),
                 vmem((2, 2, 2, rows, HEAD_DIM), BF16),
@@ -354,7 +356,7 @@
                 vmem((2, 2, rows, HEAD_DIM), BF16),
                 vmem((2, rows, HEAD_DIM), F32),
                 vmem((2, 2, rows, HEAD_DIM), F32),
-                dma((8,)),
+                dma((9,)),
                 dma((members, 2)),
                 dma((members, 2)),
                 dma((2, 2)),

time: 24.8 us -> 23.2 us (0.935)
  local copies, waits for them, and re-layouts: 2.19 us -> 1.27 us
  Pallas kernels: 21.1 us -> 20.5 us
    unnamed x4 -> x2, local copies, waits for them, and re-layouts: 2.19 us -> 1.27 us
    pallas_call x1, Pallas kernels: 21.1 us -> 20.5 us  [local(): pl.pallas_call(functools.partial(kernel, chips), out_shape=(pltpu.VMEM((r...]
where the time goes in v3:
time: 23.2 us; the launch traced here: 23 us
  Pallas kernels  20.5 us (88%)
  between operations  1.29 us (6%)
  local copies, waits for them, and re-layouts  1.27 us (5%)
    pallas_call x1, Pallas kernels, local(): pl.pallas_call(functools.partial(kernel, chips), out_shape=(pltpu.VMEM((r...  20.5 us
    unnamed x2, local copies, waits for them, and re-layouts  1.27 us

profile of v3, /device:TPU:0, one launch (start us, length us, event | category | flops | bytes accessed | tf_op | source)
XLA Modules:
  0.0 23.0 jit_solution(11508650924788152187)
XLA Ops:
  1.3 20.5 %shard_map.68 = (f32[72,256]{1,0:T(8,128)S(1)}, f32[72,256]{1,0:T(8,128)S(1)}) custom-call(s32[1]{0:T(128)S(6)} %copy.11.count_hbm, bf16[72,256]{1,0:T(8,128)(2,1)} %qs_hbm.1, bf16[72,256]{1,0:T(8,128)(2,1)} %ks_hbm.1, bf16[72,256]{1,0:T(8,128)(2,1)} %qe_hbm.1, bf16[72,256]{1,0:T(8,128)(2,1)} %ke_hbm.1), custom_call_target="tpu_custom_call" | custom-call | tf_op jit(solution)/shard_map/pallas_call | solution.py:334
  21.7 0.6 %copy.9 = f32[72,256]{1,0:T(8,128)} copy(f32[72,256]{1,0:T(8,128)S(1)} %get-tuple-element.2) | data formatting | bytes 147456
  22.4 0.6 %copy.10 = f32[72,256]{1,0:T(8,128)} copy(f32[72,256]{1,0:T(8,128)S(1)} %get-tuple-element.3) | data formatting | bytes 147456

commit v4 on v3

--- a/solution.py
+++ b/solution.py
@@ -321,6 +321,17 @@
         copy.wait_send()
 
 
+def put_out(qg_vmem, kg_vmem, qg_hbm, kg_hbm, sems):
+    copies = (
+        pltpu.make_async_copy(qg_vmem, qg_hbm, sems.at[0]),
+        pltpu.make_async_copy(kg_vmem, kg_hbm, sems.at[1]),
+    )
+    for copy in copies:
+        copy.start()
+    for copy in copies:
+        copy.wait()
+
+
 def solution(mesh):
     chips = mesh.shape["ctx"] // 2
     members = chips // 2
@@ -331,13 +342,13 @@
         dma = pltpu.SemaphoreType.DMA
         vmem = pltpu.VMEM
         any_spec = pl.BlockSpec(memory_space=pl.ANY)
-        return pl.pallas_call(
+        grads = pl.pallas_call(
             functools.partial(kernel, chips),
             out_shape=(
                 pltpu.VMEM((rows, full), F32),
                 pltpu.VMEM((rows, full), F32),
             ),
-            in_specs=[any_spec] * 5,
+            in_specs=[pl.BlockSpec(memory_space=pltpu.HBM)] * 5,
             out_specs=(pl.BlockSpec(memory_space=pltpu.VMEM),) * 2,
             scratch_shapes=[
                 pltpu.SMEM((1,), jnp.int32),
@@ -369,6 +380,13 @@
             ],
             compiler_params=pltpu.CompilerParams(collective_id=0, has_side_effects=True),
         )(text_count, query_source, key_source, query_edit, key_edit)
+        return pl.pallas_call(
+            put_out,
+            out_shape=(pltpu.HBM((rows, full), F32),) * 2,
+            in_specs=[pl.BlockSpec(memory_space=pltpu.VMEM)] * 2,
+            out_specs=(pl.BlockSpec(memory_space=pltpu.HBM),) * 2,
+            scratch_shapes=[dma((2,))],
+        )(*(pltpu.with_memory_space_constraint(g, pltpu.VMEM) for g in grads))
 
     spec = P(("req", "ctx"), None)
     return jax.shard_map(

time: 23.2 us -> 22.6 us (0.974)
  local copies, waits for them, and re-layouts: 1.27 us -> 0 us
  Pallas kernels: 20.5 us -> 21.1 us
    unnamed x2 -> x0, local copies, waits for them, and re-layouts: 1.27 us -> none
    pallas_call x0 -> x1, Pallas kernels: none -> 0.68 us  [local(): pl.pallas_call(put_out, out_shape=(pltpu.HBM((rows, full), F32),) * 2, in...]
where the time goes in v4:
time: 22.6 us; the launch traced here: 22.4 us
  Pallas kernels  21.1 us (93%)
  between operations  1.29 us (6%)
    pallas_call x1, Pallas kernels, local(): pl.pallas_call(functools.partial(kernel, chips), out_shape=(pltpu.VMEM((r...  20.5 us
    pallas_call x1, Pallas kernels, local(): pl.pallas_call(put_out, out_shape=(pltpu.HBM((rows, full), F32),) * 2, in...  0.68 us

profile of v4, /device:TPU:0, one launch (start us, length us, event | category | flops | bytes accessed | tf_op | source)
XLA Modules:
  0.0 22.4 jit_solution(6012043898512037635)
XLA Ops:
  1.3 20.5 %shard_map.68 = (f32[72,256]{1,0:T(8,128)S(1)}, f32[72,256]{1,0:T(8,128)S(1)}) custom-call(s32[1]{0:T(128)S(6)} %copy.7.count_hbm, bf16[72,256]{1,0:T(8,128)(2,1)} %qs_hbm.1, bf16[72,256]{1,0:T(8,128)(2,1)} %ks_hbm.1, bf16[72,256]{1,0:T(8,128)(2,1)} %qe_hbm.1, bf16[72,256]{1,0:T(8,128)(2,1)} %ke_hbm.1), custom_call_target="tpu_custom_call" | custom-call | tf_op jit(solution)/shard_map/pallas_call | solution.py:345
  21.7 0.7 %shard_map.69 = (f32[72,256]{1,0:T(8,128)}, f32[72,256]{1,0:T(8,128)}) custom-call(f32[72,256]{1,0:T(8,128)S(1)} %get-tuple-element.4.qg_vmem, f32[72,256]{1,0:T(8,128)S(1)} %get-tuple-element.5.kg_vmem), custom_call_target="tpu_custom_call" | custom-call | tf_op jit(solution)/shard_map/pallas_call | solution.py:383

commit v5 on v4

--- a/solution.py
+++ b/solution.py
@@ -19,8 +19,8 @@
     chips,
     count_hbm, qs_hbm, ks_hbm, qe_hbm, ke_hbm,
     qg_ref, kg_ref,
-    count_ref, krecv, kother, qrecv, qother, e_buf, s_buf, m_buf, st_send, st_recv,
-    kg_send, kg_recv, qg_send, qg_recv, kg_own, qg_own,
+    count_ref, krecv, kother, qrecv, qother, e_buf, s_buf, piece_stats, st_send, st_recv,
+    kg_send, kg_recv, qg_send, qg_recv, qg_own,
     load_sem, ksend_sem, krecv_sem, qsend_sem, qrecv_sem, st_sems,
     kgsend_sem, kgrecv_sem, qgsend_sem, qgrecv_sem,
 ):
@@ -45,7 +45,14 @@
         return {"ctx": chip_of(g, m) * 2 + c}
 
     def shifted(d):
-        return (member + d) % members
+        if members % 2:
+            return (member + d) % members
+        return (member // 2 + d // 2) % (members // 2) * 2 + (member + d) % 2
+
+    def sender(d):
+        if members % 2:
+            return (member + members - d) % members
+        return (member // 2 + members - d // 2) % (members // 2) * 2 + (member + d) % 2
 
     def each(n, body, init):
         if n <= 8:
@@ -126,7 +133,7 @@
     key_copy(member, other, False).start()
 
     def send_keys(d, carry):
-        m = shifted(d + 1)
+        m = shifted(members - 1 - d)
         key_copy(m, core, True).start()
         key_copy(m, other, False).start()
         return carry
@@ -153,10 +160,6 @@
     lane_chip = jnp.where(piece < 2, chip_of(0, member), chip_of(1, member))
     row_place = (lane_chip * 2 + piece % 2) * rows + lane % rows
     row_weight = jnp.where(valid(row_place), 2.0 * weight, 0.0)
-
-    def keys(m, which):
-        pieces = [krecv[m, c, which].astype(F32) for c in (0, 1)]
-        return jnp.concatenate(pieces, axis=0).astype(BF16)
 
     def merge(a, b):
         me1, le1, ms1, ls1, sq1, cr1 = a
@@ -171,37 +174,47 @@
             cr1 * fe1 * fs1 + cr2 * fe2 * fs2,
         )
 
-    def powers(m, which, q, key_valid, buf):
+    def powers(k, keys, q, key_valid, buf):
         scores = lax.dot_general(
-            keys(m, which), q, (((1,), (1,)), ((), ())), preferred_element_type=F32
+            keys, q, (((1,), (1,)), ((), ())), preferred_element_type=F32
         ) * scale
         scores = jnp.where(key_valid, scores, MASKED)
         top = jnp.max(scores, axis=0, keepdims=True)
         power = jnp.where(key_valid, jnp.exp(scores - top), 0.0)
-        buf[m] = power
-        m_buf[m, which:which + 1] = top
+        buf[k] = power
         return top, power, jnp.sum(power, axis=0, keepdims=True)
 
-    def score_chunk(m, stats):
-        place = chip_of(group, m) * (2 * rows) + lax.broadcasted_iota(jnp.int32, (2 * rows, 1), 0)
+    def score_piece(k, m, c):
+        place = (chip_of(group, m) * 2 + c) * rows + lax.broadcasted_iota(jnp.int32, (rows, 1), 0)
         key_valid = valid(place)
-        m_s, s_pow, l_s = powers(m, 0, q_source, key_valid, s_buf)
-        m_e, e_pow, l_e = powers(m, 1, q_edit, key_valid, e_buf)
+        m_s, s_pow, l_s = powers(k, krecv[m, c, 0], q_source, key_valid, s_buf)
+        m_e, e_pow, l_e = powers(k, krecv[m, c, 1], q_edit, key_valid, e_buf)
         sq = jnp.sum(e_pow * e_pow, axis=0, keepdims=True)
         cr = jnp.sum(e_pow * s_pow, axis=0, keepdims=True)
-        new = (m_e, l_e, m_s, l_s, sq, cr)
-        return new if stats is None else merge(stats, new)
-
+        for i, value in enumerate((m_e, l_e, m_s, l_s, sq, cr)):
+            piece_stats[i, pl.ds(k, 1)] = value
+
+    score_piece(0, member, core)
     key_arrival(member, other).wait_recv()
-    stats = score_chunk(member, None)
-
-    def far_chunk(d, stats):
-        m = shifted(members - 1 - d)
-        key_arrival(m, core).wait_recv()
-        key_arrival(m, other).wait_recv()
-        return score_chunk(m, stats)
-
-    stats = each(members - 1, far_chunk, stats)
+    score_piece(1, member, other)
+
+    def far_scores(d, carry):
+        m = sender(d + 1)
+        for i, c in enumerate((core, other)):
+            key_arrival(m, c).wait_recv()
+            score_piece(2 * (d + 1) + i, m, c)
+        return carry
+
+    each(members - 1, far_scores, 0)
+    tops_e, tops_s = piece_stats[0], piece_stats[2]
+    m_e, m_s = jnp.max(tops_e, axis=0, keepdims=True), jnp.max(tops_s, axis=0, keepdims=True)
+    f_e, f_s = jnp.exp(tops_e - m_e), jnp.exp(tops_s - m_s)
+    stats = (
+        m_e, jnp.sum(piece_stats[1] * f_e, axis=0, keepdims=True),
+        m_s, jnp.sum(piece_stats[3] * f_s, axis=0, keepdims=True),
+        jnp.sum(piece_stats[4] * (f_e * f_e), axis=0, keepdims=True),
+        jnp.sum(piece_stats[5] * (f_e * f_s), axis=0, keepdims=True),
+    )
 
     for i, value in enumerate(stats):
         st_send[i:i + 1] = value
@@ -215,6 +228,8 @@
     stat_copy.wait_recv()
     m_e, l_e, m_s, l_s, sq, cr = merge(stats, tuple(st_recv[i:i + 1] for i in range(6)))
     inv_e, inv_s = 1.0 / l_e, 1.0 / l_s
+    piece_stats[1] = jnp.exp(tops_e - m_e) * inv_e
+    piece_stats[3] = jnp.exp(tops_s - m_s) * inv_s
     delta = row_weight * (sq * inv_e * inv_e - cr * inv_e * inv_s)
 
     def kg_copy(m, c):
@@ -245,29 +260,35 @@
             device_id=dev(g, member, c),
         )
 
-    def grad_chunk(m, q_total):
-        prob_e = e_buf[m] * (jnp.exp(m_buf[m, 1:2] - m_e) * inv_e)
-        prob_s = s_buf[m] * (jnp.exp(m_buf[m, 0:1] - m_s) * inv_s)
-        grad = (prob_e * (row_weight * (prob_e - prob_s) - delta)).astype(BF16)
+    def grad_chunk(d, m, q_total):
+        grads, keys = [], []
+        for i, c in enumerate((core, other)):
+            k = 2 * d + i
+            prob_e = e_buf[k] * piece_stats[1, pl.ds(k, 1)]
+            prob_s = s_buf[k] * piece_stats[3, pl.ds(k, 1)]
+            grads.append(prob_e * (row_weight * (prob_e - prob_s) - delta))
+            keys.append(krecv[m, c, 1].astype(F32))
+        grad = jnp.concatenate(grads, axis=0).astype(BF16)
         k_part = jnp.dot(grad, q_edit, preferred_element_type=F32) * scale
         q_part = lax.dot_general(
-            keys(m, 1), grad, (((0,), (0,)), ((), ())), preferred_element_type=F32
+            jnp.concatenate(keys, axis=0).astype(BF16), grad,
+            (((0,), (0,)), ((), ())), preferred_element_type=F32,
         )
         return k_part, q_part if q_total is None else q_total + q_part
 
     def far_grad(d, q_total):
-        m = shifted(members - 1 - d)
-        k_part, q_total = grad_chunk(m, q_total)
-        for c in (0, 1):
-            kg_send[m, c] = k_part[c * rows:(c + 1) * rows].astype(BF16)
+        d = members - 1 - d
+        m = sender(d)
+        k_part, q_total = grad_chunk(d, m, q_total)
+        for i, c in enumerate((core, other)):
+            kg_send[m, c] = k_part[i * rows:(i + 1) * rows].astype(BF16)
             kg_copy(m, c).start()
         return q_total
 
     q_total = each(members - 1, far_grad, jnp.zeros((HEAD_DIM, width), F32))
-    k_part, q_total = grad_chunk(member, q_total)
-    for c in (0, 1):
-        kg_own[c] = k_part[c * rows:(c + 1) * rows]
-    kg_send[member, other] = kg_own[other].astype(BF16)
+    k_part, q_total = grad_chunk(0, member, q_total)
+    kg_mine = k_part[:rows]
+    kg_send[member, other] = k_part[rows:].astype(BF16)
     kg_copy(member, other).start()
 
     q_rows = q_total.T * scale
@@ -293,7 +314,7 @@
         kg_arrival(m, other).wait_recv()
         return mine + kg_recv[m, core].astype(F32), theirs + kg_recv[m, other].astype(F32)
 
-    sums = each(members - 1, add_far, (kg_own[core], kg_recv[member, other].astype(F32)))
+    sums = each(members - 1, add_far, (kg_mine, kg_recv[member, other].astype(F32)))
     put(kg_ref, *sums)
 
     qg_arrival(group, other).wait_recv()
@@ -356,16 +377,15 @@
                 vmem((2, rows, HEAD_DIM), BF16),
                 vmem((2, 2, 2, rows, HEAD_DIM), BF16),
                 vmem((2, rows, HEAD_DIM), BF16),
-                vmem((members, 2 * rows, width), F32),
-                vmem((members, 2 * rows, width), F32),
-                vmem((members, 8, width), F32),
+                vmem((2 * members, rows, width), F32),
+                vmem((2 * members, rows, width), F32),
+                vmem((6, 2 * members, width), F32),
                 vmem((8, width), F32),
                 vmem((8, width), F32),
                 vmem((members, 2, rows, HEAD_DIM), BF16),
                 vmem((members, 2, rows, HEAD_DIM), BF16),
                 vmem((2, 2, rows, HEAD_DIM), BF16),
                 vmem((2, 2, rows, HEAD_DIM), BF16),
-                vmem((2, rows, HEAD_DIM), F32),
                 vmem((2, 2, rows, HEAD_DIM), F32),
                 dma((9,)),
                 dma((members, 2)),

time: 22.6 us -> 23 us (1.018)
  Pallas kernels: 21.1 us -> 21.6 us
    pallas_call x1, Pallas kernels: 20.5 us -> 20.9 us  [local(): pl.pallas_call(functools.partial(kernel, chips), out_shape=(pltpu.VMEM((r...]
where the time goes in v5:
time: 23 us; the launch traced here: 22.8 us
  Pallas kernels  21.6 us (94%)
  between operations  1.29 us (6%)
    pallas_call x1, Pallas kernels, local(): pl.pallas_call(functools.partial(kernel, chips), out_shape=(pltpu.VMEM((r...  20.9 us
    pallas_call x1, Pallas kernels, local(): pl.pallas_call(put_out, out_shape=(pltpu.HBM((rows, full), F32),) * 2, in...  0.68 us

profile of v5, /device:TPU:0, one launch (start us, length us, event | category | flops | bytes accessed | tf_op | source)
XLA Modules:
  0.0 22.8 jit_solution(7456627012079757191)
XLA Ops:
  1.3 20.9 %shard_map.68 = (f32[72,256]{1,0:T(8,128)S(1)}, f32[72,256]{1,0:T(8,128)S(1)}) custom-call(s32[1]{0:T(128)S(6)} %copy.7.count_hbm, bf16[72,256]{1,0:T(8,128)(2,1)} %qs_hbm.1, bf16[72,256]{1,0:T(8,128)(2,1)} %ks_hbm.1, bf16[72,256]{1,0:T(8,128)(2,1)} %qe_hbm.1, bf16[72,256]{1,0:T(8,128)(2,1)} %ke_hbm.1), custom_call_target="tpu_custom_call" | custom-call | tf_op jit(solution)/shard_map/pallas_call | solution.py:366
  22.2 0.7 %shard_map.69 = (f32[72,256]{1,0:T(8,128)}, f32[72,256]{1,0:T(8,128)}) custom-call(f32[72,256]{1,0:T(8,128)S(1)} %get-tuple-element.4.qg_vmem, f32[72,256]{1,0:T(8,128)S(1)} %get-tuple-element.5.kg_vmem), custom_call_target="tpu_custom_call" | custom-call | tf_op jit(solution)/shard_map/pallas_call | solution.py:403

commit v6 on v5

--- a/solution.py
+++ b/solution.py
@@ -49,6 +49,9 @@
             return (member + d) % members
         return (member // 2 + d // 2) % (members // 2) * 2 + (member + d) % 2
 
+    def cycled(d):
+        return (member + d) % members
+
     def sender(d):
         if members % 2:
             return (member + members - d) % members
@@ -133,7 +136,7 @@
     key_copy(member, other, False).start()
 
     def send_keys(d, carry):
-        m = shifted(members - 1 - d)
+        m = cycled(d + 1)
         key_copy(m, core, True).start()
         key_copy(m, other, False).start()
         return carry
@@ -165,8 +168,8 @@
         me1, le1, ms1, ls1, sq1, cr1 = a
         me2, le2, ms2, ls2, sq2, cr2 = b
         m_e, m_s = jnp.maximum(me1, me2), jnp.maximum(ms1, ms2)
-        fe1, fe2 = jnp.exp(me1 - m_e), jnp.exp(me2 - m_e)
-        fs1, fs2 = jnp.exp(ms1 - m_s), jnp.exp(ms2 - m_s)
+        fe1, fe2 = jnp.exp2(me1 - m_e), jnp.exp2(me2 - m_e)
+        fs1, fs2 = jnp.exp2(ms1 - m_s), jnp.exp2(ms2 - m_s)
         return (
             m_e, le1 * fe1 + le2 * fe2,
             m_s, ls1 * fs1 + ls2 * fs2,
@@ -177,10 +180,10 @@
     def powers(k, keys, q, key_valid, buf):
         scores = lax.dot_general(
             keys, q, (((1,), (1,)), ((), ())), preferred_element_type=F32
-        ) * scale
+        ) * (scale * math.log2(math.e))
         scores = jnp.where(key_valid, scores, MASKED)
         top = jnp.max(scores, axis=0, keepdims=True)
-        power = jnp.where(key_valid, jnp.exp(scores - top), 0.0)
+        power = jnp.exp2(scores - top)
         buf[k] = power
         return top, power, jnp.sum(power, axis=0, keepdims=True)
 
@@ -199,16 +202,17 @@
     score_piece(1, member, other)
 
     def far_scores(d, carry):
-        m = sender(d + 1)
+        m = cycled(members - 1 - d)
+        for c in (core, other):
+            key_arrival(m, c).wait_recv()
         for i, c in enumerate((core, other)):
-            key_arrival(m, c).wait_recv()
             score_piece(2 * (d + 1) + i, m, c)
         return carry
 
     each(members - 1, far_scores, 0)
     tops_e, tops_s = piece_stats[0], piece_stats[2]
     m_e, m_s = jnp.max(tops_e, axis=0, keepdims=True), jnp.max(tops_s, axis=0, keepdims=True)
-    f_e, f_s = jnp.exp(tops_e - m_e), jnp.exp(tops_s - m_s)
+    f_e, f_s = jnp.exp2(tops_e - m_e), jnp.exp2(tops_s - m_s)
     stats = (
         m_e, jnp.sum(piece_stats[1] * f_e, axis=0, keepdims=True),
         m_s, jnp.sum(piece_stats[3] * f_s, axis=0, keepdims=True),
@@ -228,8 +232,8 @@
     stat_copy.wait_recv()
     m_e, l_e, m_s, l_s, sq, cr = merge(stats, tuple(st_recv[i:i + 1] for i in range(6)))
     inv_e, inv_s = 1.0 / l_e, 1.0 / l_s
-    piece_stats[1] = jnp.exp(tops_e - m_e) * inv_e
-    piece_stats[3] = jnp.exp(tops_s - m_s) * inv_s
+    piece_stats[1] = jnp.exp2(tops_e - m_e) * inv_e
+    piece_stats[3] = jnp.exp2(tops_s - m_s) * inv_s
     delta = row_weight * (sq * inv_e * inv_e - cr * inv_e * inv_s)
 
     def kg_copy(m, c):
@@ -278,18 +282,16 @@
 
     def far_grad(d, q_total):
         d = members - 1 - d
-        m = sender(d)
+        m = cycled(members - d)
         k_part, q_total = grad_chunk(d, m, q_total)
         for i, c in enumerate((core, other)):
             kg_send[m, c] = k_part[i * rows:(i + 1) * rows].astype(BF16)
-            kg_copy(m, c).start()
         return q_total
 
     q_total = each(members - 1, far_grad, jnp.zeros((HEAD_DIM, width), F32))
     k_part, q_total = grad_chunk(0, member, q_total)
     kg_mine = k_part[:rows]
     kg_send[member, other] = k_part[rows:].astype(BF16)
-    kg_copy(member, other).start()
 
     q_rows = q_total.T * scale
     for g in (0, 1):
@@ -300,6 +302,15 @@
     qg_copy(1 - group, core).start()
     qg_copy(1 - group, other).start()
     qg_copy(group, other).start()
+
+    def send_kg(d, carry):
+        m = cycled(members - 1 - d)
+        for c in (core, other):
+            kg_copy(m, c).start()
+        return carry
+
+    each(members - 1, send_kg, 0)
+    kg_copy(member, other).start()
 
     def put(ref, mine, theirs):
         ref[:, :HEAD_DIM] = jnp.where(core == 0, mine, theirs)

time: 23 us -> 22.5 us (0.978)
  Pallas kernels: 21.6 us -> 21.1 us
    pallas_call x1, Pallas kernels: 20.9 us -> 20.4 us  [local(): pl.pallas_call(functools.partial(kernel, chips), out_shape=(pltpu.VMEM((r...]
where the time goes in v6:
time: 22.5 us; the launch traced here: 22.4 us
  Pallas kernels  21.1 us (94%)
  between operations  1.29 us (6%)
    pallas_call x1, Pallas kernels, local(): pl.pallas_call(functools.partial(kernel, chips), out_shape=(pltpu.VMEM((r...  20.4 us
    pallas_call x1, Pallas kernels, local(): pl.pallas_call(put_out, out_shape=(pltpu.HBM((rows, full), F32),) * 2, in...  0.68 us

profile of v6, /device:TPU:0, one launch (start us, length us, event | category | flops | bytes accessed | tf_op | source)
XLA Modules:
  0.0 22.4 jit_solution(11434904759424496967)
XLA Ops:
  1.3 20.4 %shard_map.68 = (f32[72,256]{1,0:T(8,128)S(1)}, f32[72,256]{1,0:T(8,128)S(1)}) custom-call(s32[1]{0:T(128)S(6)} %copy.7.count_hbm, bf16[72,256]{1,0:T(8,128)(2,1)} %qs_hbm.1, bf16[72,256]{1,0:T(8,128)(2,1)} %ks_hbm.1, bf16[72,256]{1,0:T(8,128)(2,1)} %qe_hbm.1, bf16[72,256]{1,0:T(8,128)(2,1)} %ke_hbm.1), custom_call_target="tpu_custom_call" | custom-call | tf_op jit(solution)/shard_map/pallas_call | solution.py:377
  21.7 0.7 %shard_map.69 = (f32[72,256]{1,0:T(8,128)}, f32[72,256]{1,0:T(8,128)}) custom-call(f32[72,256]{1,0:T(8,128)S(1)} %get-tuple-element.4.qg_vmem, f32[72,256]{1,0:T(8,128)S(1)} %get-tuple-element.5.kg_vmem), custom_call_target="tpu_custom_call" | custom-call | tf_op jit(solution)/shard_map/pallas_call | solution.py:414
